TPU v7x, 128 devices: a whole 4x4x4 slice. The times are simulated.
128 devices in a mesh: dp: 16 (over x_lo, y, core), shard: 8 (over x_hi, z).
Axes of the slice: x: 4 (x_hi: 2, x_lo: 2; x = x_hi * 2 + x_lo), y: 4, z: 4, core: 2. Of those that a mesh axis runs over, the one named last changes fastest.
Arguments:
- grad_parts: bfloat16 [16, 16, 1024, 1024], P('dp', None, 'shard'), may hold values from -6 to 6
- first_moment: float32 [16384, 1024], P(('dp', 'shard')), may hold values from -6 to 6
- second_moment: float32 [16384, 1024], P(('dp', 'shard')), may hold values from 0.1 to 16
- master: float32 [16384, 1024], P(('dp', 'shard')), may hold values from -6 to 6
- old_map: int32 [16384], replicated, may hold values from 0 to 16383, as said below
- new_map: int32 [16384], replicated, may hold values from 0 to 16383, as said below
Outputs:
- new_first: float32 [16384, 1024], P(('dp', 'shard'))
- new_second: float32 [16384, 1024], P(('dp', 'shard'))
- new_master: float32 [16384, 1024], P(('dp', 'shard'))
- weights_half: bfloat16 [16384, 1024], P('dp')
Inputs may be any that keep to these rules, and one draw needn't show every extreme that they name: old_map is a permutation of the 16384 block numbers. Row r of either layout belongs to device r // 128. Of the blocks that one device holds in the old layout, exactly one belongs to each device in the new layout. new_map is a permutation of the 16384 block numbers, with the property stated for old_map.
All inputs are finite; a program needn't handle non-finite values.
Results may differ from a plain program's by a relative error of at most 0.0085.
Values may be sent and summed in bfloat16 or wider, within the bound.
A program may use at most 64 MiB of HBM per device.

v0:
```python
import jax
import jax.numpy as jnp
from jax import lax
from jax.sharding import PartitionSpec as P

beta_one = 0.9
beta_two = 0.95
learning_rate = 0.05
decay_rate = 0.1
epsilon = 1e-08
step_count = 4


def adamw(moment_one, moment_two, weights, gradient):
    new_one = beta_one * moment_one + (1.0 - beta_one) * gradient
    new_two = beta_two * moment_two + (1.0 - beta_two) * gradient * gradient
    unbiased_one = new_one / (1.0 - beta_one**step_count)
    unbiased_two = new_two / (1.0 - beta_two**step_count)
    updated = weights - learning_rate * (
        unbiased_one / (jnp.sqrt(unbiased_two) + epsilon) + decay_rate * weights
    )
    return (new_one, new_two, updated)


def owner_table(blocks, mapping, device_count, span):
    grid = mapping.reshape(device_count, span)
    found = jnp.any(blocks[:, None, None] == grid[None, :, :], axis=2)
    return found.astype(jnp.float32)


def local(grad_parts, first_moment, second_moment, master, old_map, new_map):
    groups = lax.axis_size("dp")
    shard_width = lax.axis_size("shard")
    device_count = groups * shard_width
    my_index = lax.axis_index("dp") * shard_width + lax.axis_index("shard")
    span = first_moment.shape[0]
    block_len = first_moment.shape[1]
    summed_grad = lax.psum_scatter(
        grad_parts[0].astype(jnp.float32).astype(jnp.bfloat16),
        "dp",
        scatter_dimension=0,
        tiled=True,
    ).astype(jnp.float32)[0]
    local_blocks = lax.dynamic_slice_in_dim(old_map, my_index * span, span)
    route = owner_table(local_blocks, new_map, device_count, span)
    packed = jnp.stack([first_moment, second_moment, master], axis=1).reshape(span, 3 * block_len)
    outgoing = jnp.dot(
        route.T, packed, precision=lax.Precision.HIGHEST, preferred_element_type=jnp.float32
    )
    outgoing = outgoing.reshape(device_count, 3, block_len)
    incoming = lax.all_to_all(outgoing, ("dp", "shard"), split_axis=0, concat_axis=0, tiled=True)
    incoming = incoming.reshape(device_count, 3 * block_len)
    wanted = lax.dynamic_slice_in_dim(new_map, my_index * span, span)
    pick = owner_table(wanted, old_map, device_count, span)
    states = jnp.dot(
        pick, incoming, precision=lax.Precision.HIGHEST, preferred_element_type=jnp.float32
    )
    states = states.reshape(span, 3, block_len)
    new_one, new_two, updated = adamw(states[:, 0], states[:, 1], states[:, 2], summed_grad)
    gathered = lax.all_gather(updated.astype(jnp.bfloat16), "shard", axis=0, tiled=True)
    return (new_one, new_two, updated, gathered)


def solution(mesh):
    placed = (
        P("dp", None, "shard", None),
        P(("dp", "shard"), None),
        P(("dp", "shard"), None),
        P(("dp", "shard"), None),
        P(),
        P(),
    )
    return jax.shard_map(
        local,
        mesh=mesh,
        in_specs=placed,
        out_specs=(
            P(("dp", "shard"), None),
            P(("dp", "shard"), None),
            P(("dp", "shard"), None),
            P("dp", None),
        ),
        check_vma=False,
    )
```

profile of v0, /device:TPU:1, one launch (start us, length us, event | category | flops | bytes accessed | tf_op | source)
XLA Modules:
  0.0 161.5 jit_solution(11646434920903755506)
XLA Ops:
  7.2 0.0 reduce-scatter.2.cloned.1.call-start
  7.2 0.0 copy-start
  7.2 0.0 copy-start.1
  7.2 0.7 reduce-scatter.2.cloned.1.call-update
  7.9 0.0 copy-start.2
  7.9 0.3 copy-done
  8.3 0.0 copy-start.4
  8.3 0.0 copy-start.3
  8.3 0.2 copy.19
  8.5 0.0 copy-done.1
  8.5 0.2 copy.20
  8.7 0.4 copy-done.2
  9.0 0.2 copy.21
  9.2 0.0 copy-done.4
  9.2 0.1 dynamic_slice.7
  9.3 0.0 copy-done.3
  9.3 2.4 %compare_reduce_fusion = pred[128,128]{1,0:T(8,128)(4,1)S(1)} fusion(s32[128,128]{1,0:T(8,128)S(1)} %bitcast.54, s32[128]{0:T(128)S(1)} %dynamic_slice.7), kind=kLoop, calls=%fused_computation | loop fusion | flops 4177920 | bytes 82432 | tf_op jit(solution)/shard_map/reduce_or | solution.py:27
  11.7 1.0 fusion
  12.7 2.4 %copy.23 = f32[128,3,1024]{2,1,0:T(4,128)} copy(f32[128,3,1024]{2,0,1:T(8,128)S(1)} %fusion) | data formatting | bytes 3145728 | tf_op jit(solution)/shard_map/dot_general | solution.py:47
  15.1 11.5 %all-to-all-start = ((f32[128,3,1024]{2,1,0:T(4,128)}), f32[128,3,1024]{2,1,0:T(4,128)S(1)}, u32[]{:S(2)}, u32[]{:S(2)}) async-start(f32[128,3,1024]{2,1,0:T(4,128)} %copy.23), calls=%async_computation | async-start | bytes 4194304 | tf_op jit(solution)/shard_map/all_to_all | solution.py:51
  26.6 0.0 all-gather.2.cloned.1.call-start
  26.6 0.1 dynamic_slice.6
  26.7 2.4 %compare_reduce_fusion.1 = pred[128,128]{1,0:T(8,128)(4,1)S(1)} fusion(s32[128,128]{1,0:T(8,128)S(1)} %bitcast.55, s32[128]{0:T(128)S(1)} %dynamic_slice.6), kind=kLoop, calls=%fused_computation.1 | loop fusion | flops 4177920 | bytes 82432 | tf_op jit(solution)/shard_map/reduce_or | solution.py:27
  29.1 30.2 %all-to-all-done = f32[128,3,1024]{2,1,0:T(4,128)S(1)} async-done(((f32[128,3,1024]{2,1,0:T(4,128)}), f32[128,3,1024]{2,1,0:T(4,128)S(1)}, u32[]{:S(2)}, u32[]{:S(2)}) %all-to-all-start) | async-done | bytes 1572896 | tf_op jit(solution)/shard_map/all_to_all | solution.py:51
  59.3 1.6 %copy.24 = f32[128,3,1024]{0,2,1:T(8,128)} copy(f32[128,3,1024]{2,1,0:T(4,128)S(1)} %all-to-all-done) | data formatting | bytes 3145728 | tf_op jit(solution)/shard_map/all_to_all | solution.py:51
  61.0 2.4 %fusion.5 = f32[128,3,1024]{2,0,1:T(8,128)S(1)} fusion(f32[128,3,1024]{0,2,1:T(8,128)} %copy.24, pred[128,128]{1,0:T(8,128)(4,1)S(1)} %compare_reduce_fusion.1), kind=kOutput, calls=%fused_computation.8 | convolution fusion | flops 603979776 | bytes 3162112 | tf_op jit(solution)/shard_map/dot_general | solution.py:55
  63.3 29.1 %reduce-scatter.2.cloned.1.call-done = bf16[1,128,1024]{2,1,0:T(8,128)(2,1)} async-done(((bf16[16,128,1024]{2,1,0:T(8,128)(2,1)}), bf16[1,128,1024]{2,1,0:T(8,128)(2,1)}) %reduce-scatter.2.cloned.1.call-update) | async-done | bytes 262160 | tf_op jit(solution)/shard_map/reduce_scatter | solution.py:38
  92.4 2.4 %fusion.14 = (bf16[128,1024]{1,0:T(8,128)(2,1)}, f32[128,1024]{1,0:T(8,128)}, f32[128,1024]{1,0:T(8,128)}, f32[128,1024]{1,0:T(8,128)}) fusion(f32[128,3,1024]{2,0,1:T(8,128)S(1)} %fusion.5, bf16[1,128,1024]{2,1,0:T(8,128)(2,1)} %reduce-scatter.2.cloned.1.call-done), kind=kLoop, calls=%fused_computation.24 | loop fusion | flops 2228224 | bytes 3670016 | tf_op jit(solution)/shard_map/convert_element_type | solution.py:60
  94.8 0.0 all-gather.2.cloned.1.call-update
  94.8 56.8 %all-gather.2.cloned.1.call-done = bf16[1024,1024]{1,0:T(8,128)(2,1)} async-done(((bf16[128,1024]{1,0:T(8,128)(2,1)}), bf16[1024,1024]{1,0:T(8,128)(2,1)}) %all-gather.2.cloned.1.call-update) | async-done | bytes 2097168 | tf_op jit(solution)/shard_map/all_gather | solution.py:60
  151.6 3.1 %copy.28 = bf16[1024,1024]{1,0:T(8,128)(2,1)} copy(bf16[1024,1024]{1,0:T(8,128)(2,1)} %all-gather.2.cloned.1.call-done) | data formatting | bytes 4194304
Async XLA Ops:
  7.2 85.2 %reduce-scatter.2.cloned.1.call-start = ((), (), s32[]{:S(2)}) async-start(), calls=%async_computation.2 | async-start | bytes 4456448 | tf_op jit(solution)/shard_map/reduce_scatter | solution.py:38
  7.2 1.0 copy-start
  7.2 1.2 copy-start.1
  7.9 1.1 copy-start.2
  8.3 1.0 copy-start.4
  8.3 1.1 copy-start.3
  15.1 44.3 %all-to-all-start = ((f32[128,3,1024]{2,1,0:T(4,128)}), f32[128,3,1024]{2,1,0:T(4,128)S(1)}, u32[]{:S(2)}, u32[]{:S(2)}) async-start(f32[128,3,1024]{2,1,0:T(4,128)} %copy.23), calls=%async_computation | async-start | bytes 4194304 | tf_op jit(solution)/shard_map/all_to_all | solution.py:51
  26.6 125.0 %all-gather.2.cloned.1.call-start = ((), (), s32[]{:S(2)}) async-start(), calls=%async_computation.3 | async-start | bytes 2359296 | tf_op jit(solution)/shard_map/all_gather | solution.py:60
Sparse Core Ops, SparseCore 0:
  10.4 81.9 reduce-scatter.1
  95.3 56.2 all-gather.1
where the time goes:
time: 162 us
  waiting for transfers between devices  117 us (72%)
  between operations  14.1 us (9%)
  starting transfers between devices  11.6 us (7%)
  local copies, waits for them, and re-layouts  8.54 us (5%)
  other arithmetic  7.22 us (4%)
  matrix products  3.3 us (2%)
    all_gather x1, waiting for transfers between devices, local(): lax.all_gather(updated.astype(jnp.bfloat16), 'shard', axis=0, tiled=True)  56.8 us
    all_to_all x1, waiting for transfers between devices, local(): lax.all_to_all(outgoing, ('dp', 'shard'), split_axis=0, concat_axis=0, ti...  30.2 us
    reduce_scatter x1, waiting for transfers between devices, local(): lax.psum_scatter(grad_parts[0].astype(jnp.float32).astype(jnp.bfloat16),...  29.1 us
    all_to_all x1, starting transfers between devices, local(): lax.all_to_all(outgoing, ('dp', 'shard'), split_axis=0, concat_axis=0, ti...  11.5 us
    reduce_or x2, other arithmetic, owner_table(): found = jnp.any(blocks[:, None, None] == grid[None, :, :], axis=2)  4.78 us
    unnamed x14, local copies, waits for them, and re-layouts  4.36 us
  transfers between devices with their start and end apart: 3, of which 3 were waited for; matrix products, arithmetic and copies ran while one was open for 8% of the time, Pallas kernels for 0%

commit v1 on v0

--- a/solution.py
+++ b/solution.py
@@ -57,7 +57,12 @@
     )
     states = states.reshape(span, 3, block_len)
     new_one, new_two, updated = adamw(states[:, 0], states[:, 1], states[:, 2], summed_grad)
-    gathered = lax.all_gather(updated.astype(jnp.bfloat16), "shard", axis=0, tiled=True)
+    gathered = jnp.concatenate(
+        lax.all_to_all(
+            jnp.stack([updated.astype(jnp.bfloat16)] * lax.axis_size("shard")), "shard", 0, 0
+        ),
+        axis=0,
+    )
     return (new_one, new_two, updated, gathered)
 
 

time: 162 us -> 139 us (0.86)
  waiting for transfers between devices: 117 us -> 83.1 us
  starting transfers between devices: 11.6 us -> 19 us
    all_gather x1 -> x0, waiting for transfers between devices: 56.8 us -> none  [local(): lax.all_gather(updated.astype(jnp.bfloat16), 'shard', axis=0, tiled=True)]
    all_to_all x0 -> x1, waiting for transfers between devices: none -> 23.1 us  [local(): lax.all_to_all(jnp.stack([updated.astype(jnp.bfloat16)] * lax.axis_size('...]
    all_to_all x0 -> x1, starting transfers between devices: none -> 7.45 us  [local(): lax.all_to_all(jnp.stack([updated.astype(jnp.bfloat16)] * lax.axis_size('...]
    convert_element_type x1 -> x0, other arithmetic: 2.44 us -> none  [local(): updated.astype(jnp.bfloat16)]
    unnamed x14 -> x16, local copies, waits for them, and re-layouts: 4.36 us -> 4.36 us
  transfers between devices with their start and end apart: 3 -> 3, of which waited for: 3 -> 3; matrix products, arithmetic and copies ran while one was open for 8% -> 10% of each run, Pallas kernels for 0% -> 0%
where the time goes in v1:
time: 139 us; the launch traced here: 137 us
  waiting for transfers between devices  83.1 us (60%)
  starting transfers between devices  19 us (14%)
  between operations  14.1 us (10%)
  local copies, waits for them, and re-layouts  10.1 us (7%)
  other arithmetic  7.56 us (5%)
  matrix products  3.3 us (2%)
    all_to_all x1, waiting for transfers between devices, local(): lax.all_to_all(outgoing, ('dp', 'shard'), split_axis=0, concat_axis=0, ti...  30.3 us
    reduce_scatter x1, waiting for transfers between devices, local(): lax.psum_scatter(grad_parts[0].astype(jnp.float32).astype(jnp.bfloat16),...  29.1 us
    all_to_all x1, waiting for transfers between devices, local(): lax.all_to_all(jnp.stack([updated.astype(jnp.bfloat16)] * lax.axis_size('...  23.1 us
    all_to_all x1, starting transfers between devices, local(): lax.all_to_all(outgoing, ('dp', 'shard'), split_axis=0, concat_axis=0, ti...  11.5 us
    all_to_all x1, starting transfers between devices, local(): lax.all_to_all(jnp.stack([updated.astype(jnp.bfloat16)] * lax.axis_size('...  7.45 us
    reduce_or x2, other arithmetic, owner_table(): found = jnp.any(blocks[:, None, None] == grid[None, :, :], axis=2)  4.78 us
    unnamed x16, local copies, waits for them, and re-layouts  4.36 us
  transfers between devices with their start and end apart: 3, of which 3 were waited for; matrix products, arithmetic and copies ran while one was open for 10% of the time, Pallas kernels for 0%

profile of v1, /device:TPU:1, one launch (start us, length us, event | category | flops | bytes accessed | tf_op | source)
XLA Modules:
  0.0 137.2 jit_solution(17616249007535332194)
XLA Ops:
  7.2 0.0 reduce-scatter.2.cloned.1.call-start
  7.2 0.0 copy-start.1
  7.2 0.0 copy-start.2
  7.2 0.7 reduce-scatter.2.cloned.1.call-update
  7.9 0.0 copy-start.3
  7.9 0.3 copy-done.1
  8.3 0.0 copy-start.5
  8.3 0.0 copy-start.4
  8.3 0.2 copy.19
  8.5 0.0 copy-done.2
  8.5 0.2 copy.20
  8.7 0.4 copy-done.3
  9.0 0.2 copy.21
  9.2 0.0 copy-done.5
  9.2 0.1 dynamic_slice.7
  9.3 0.0 copy-done.4
  9.3 2.4 %compare_reduce_fusion = pred[128,128]{1,0:T(8,128)(4,1)S(1)} fusion(s32[128,128]{1,0:T(8,128)S(1)} %bitcast.88, s32[128]{0:T(128)S(1)} %dynamic_slice.7), kind=kLoop, calls=%fused_computation | loop fusion | flops 4177920 | bytes 82432 | tf_op jit(solution)/shard_map/reduce_or | solution.py:27
  11.7 1.0 fusion
  12.7 2.4 %copy.23 = f32[128,3,1024]{2,1,0:T(4,128)} copy(f32[128,3,1024]{2,0,1:T(8,128)S(1)} %fusion) | data formatting | bytes 3145728 | tf_op jit(solution)/shard_map/dot_general | solution.py:47
  15.1 11.5 %all-to-all-start = ((f32[128,3,1024]{2,1,0:T(4,128)}), f32[128,3,1024]{2,1,0:T(4,128)S(1)}, u32[]{:S(2)}, u32[]{:S(2)}) async-start(f32[128,3,1024]{2,1,0:T(4,128)} %copy.23), calls=%async_computation | async-start | bytes 4194304 | tf_op jit(solution)/shard_map/all_to_all | solution.py:51
  26.6 0.1 dynamic_slice.6
  26.6 2.4 %compare_reduce_fusion.1 = pred[128,128]{1,0:T(8,128)(4,1)S(1)} fusion(s32[128,128]{1,0:T(8,128)S(1)} %bitcast.89, s32[128]{0:T(128)S(1)} %dynamic_slice.6), kind=kLoop, calls=%fused_computation.1 | loop fusion | flops 4177920 | bytes 82432 | tf_op jit(solution)/shard_map/reduce_or | solution.py:27
  29.0 30.3 %all-to-all-done = f32[128,3,1024]{2,1,0:T(4,128)S(1)} async-done(((f32[128,3,1024]{2,1,0:T(4,128)}), f32[128,3,1024]{2,1,0:T(4,128)S(1)}, u32[]{:S(2)}, u32[]{:S(2)}) %all-to-all-start) | async-done | bytes 1572896 | tf_op jit(solution)/shard_map/all_to_all | solution.py:51
  59.3 1.6 %copy.24 = f32[128,3,1024]{0,2,1:T(8,128)} copy(f32[128,3,1024]{2,1,0:T(4,128)S(1)} %all-to-all-done) | data formatting | bytes 3145728 | tf_op jit(solution)/shard_map/all_to_all | solution.py:51
  61.0 2.4 %fusion.5 = f32[128,3,1024]{2,0,1:T(8,128)S(1)} fusion(f32[128,3,1024]{0,2,1:T(8,128)} %copy.24, pred[128,128]{1,0:T(8,128)(4,1)S(1)} %compare_reduce_fusion.1), kind=kOutput, calls=%fused_computation.8 | convolution fusion | flops 603979776 | bytes 3162112 | tf_op jit(solution)/shard_map/dot_general | solution.py:55
  63.3 29.1 %reduce-scatter.2.cloned.1.call-done = bf16[1,128,1024]{2,1,0:T(8,128)(2,1)} async-done(((bf16[16,128,1024]{2,1,0:T(8,128)(2,1)}), bf16[1,128,1024]{2,1,0:T(8,128)(2,1)}) %reduce-scatter.2.cloned.1.call-update) | async-done | bytes 262160 | tf_op jit(solution)/shard_map/reduce_scatter | solution.py:38
  92.4 1.4 %fusion.25 = bf16[128,1024]{1,0:T(8,128)(2,1)S(1)} fusion(f32[128,3,1024]{2,0,1:T(8,128)S(1)} %fusion.5, bf16[1,128,1024]{2,1,0:T(8,128)(2,1)} %reduce-scatter.2.cloned.1.call-done), kind=kLoop, calls=%fused_computation.37 | loop fusion | flops 2228224 | bytes 2097152 | tf_op jit(solution)/shard_map/stack | solution.py:62
  93.7 1.6 %stack.30 = bf16[8,128,1024]{2,1,0:T(8,128)(2,1)} broadcast(bf16[128,1024]{1,0:T(8,128)(2,1)S(1)} %fusion.25), dimensions={1,2} | broadcast | bytes 2359296 | tf_op jit(solution)/shard_map/stack | solution.py:62
  95.3 0.0 copy-start
  95.3 7.5 %all-to-all-start.1 = ((bf16[8,128,1024]{2,1,0:T(8,128)(2,1)}), bf16[8,128,1024]{2,1,0:T(8,128)(2,1)}, u32[]{:S(2)}, u32[]{:S(2)}) async-start(bf16[8,128,1024]{2,1,0:T(8,128)(2,1)} %stack.30), calls=%async_computation.2 | async-start | bytes 4194304 | tf_op jit(solution)/shard_map/all_to_all | solution.py:61
  102.8 0.0 copy-done
  102.8 1.4 %bitcast_subtract_fusion = (f32[128,1024]{1,0:T(8,128)}, f32[128,1024]{1,0:T(8,128)}, f32[128,1024]{1,0:T(8,128)}) fusion(f32[128,3,1024]{2,0,1:T(8,128)S(1)} %fusion.5, bf16[1,128,1024]{2,1,0:T(8,128)(2,1)S(1)} %copy-done), kind=kLoop, calls=%fused_computation.32 | loop fusion | flops 2097152 | bytes 3407872 | tf_op jit(solution)/shard_map/sub | solution.py:19
  104.2 23.1 %all-to-all-done.1 = bf16[8,128,1024]{2,1,0:T(8,128)(2,1)} async-done(((bf16[8,128,1024]{2,1,0:T(8,128)(2,1)}), bf16[8,128,1024]{2,1,0:T(8,128)(2,1)}, u32[]{:S(2)}, u32[]{:S(2)}) %all-to-all-start.1) | async-done | bytes 2097184 | tf_op jit(solution)/shard_map/all_to_all | solution.py:61
  127.3 3.1 %copy.28 = bf16[1024,1024]{1,0:T(8,128)(2,1)} copy(bf16[1024,1024]{1,0:T(8,128)(2,1)} %bitcast.22) | data formatting | bytes 4194304
Async XLA Ops:
  7.2 85.2 %reduce-scatter.2.cloned.1.call-start = ((), (), s32[]{:S(2)}) async-start(), calls=%async_computation.3 | async-start | bytes 4456448 | tf_op jit(solution)/shard_map/reduce_scatter | solution.py:38
  7.2 1.0 copy-start.1
  7.2 1.2 copy-start.2
  7.9 1.1 copy-start.3
  8.3 1.0 copy-start.5
  8.3 1.1 copy-start.4
  15.1 44.3 %all-to-all-start = ((f32[128,3,1024]{2,1,0:T(4,128)}), f32[128,3,1024]{2,1,0:T(4,128)S(1)}, u32[]{:S(2)}, u32[]{:S(2)}) async-start(f32[128,3,1024]{2,1,0:T(4,128)} %copy.23), calls=%async_computation | async-start | bytes 4194304 | tf_op jit(solution)/shard_map/all_to_all | solution.py:51
  95.3 7.5 %copy-start = (bf16[1,128,1024]{2,1,0:T(8,128)(2,1)S(1)}, bf16[1,128,1024]{2,1,0:T(8,128)(2,1)}, u32[]{:S(2)}) copy-start(bf16[1,128,1024]{2,1,0:T(8,128)(2,1)} %reduce-scatter.2.cloned.1.call-done) | copy-start | bytes 786436
  95.3 31.9 %all-to-all-start.1 = ((bf16[8,128,1024]{2,1,0:T(8,128)(2,1)}), bf16[8,128,1024]{2,1,0:T(8,128)(2,1)}, u32[]{:S(2)}, u32[]{:S(2)}) async-start(bf16[8,128,1024]{2,1,0:T(8,128)(2,1)} %stack.30), calls=%async_computation.2 | async-start | bytes 4194304 | tf_op jit(solution)/shard_map/all_to_all | solution.py:61
Sparse Core Ops, SparseCore 0:
  10.4 81.9 reduce-scatter.1
